TPU v7x, 256 devices: a whole 4x4x8 slice. The times are simulated.
256 devices in a mesh: inst: 8 (over y_hi, x), space: 32 (over z, y_lo, core).
Axes of the slice: x: 4, y: 4 (y_hi: 2, y_lo: 2; y = y_hi * 2 + y_lo), z: 8, core: 2. Of those that a mesh axis runs over, the one named last changes fastest.
Arguments:
- psi_start: float32 [5, 8, 256, 1024], P(None, 'inst', 'space'), may hold values from -6 to 6
- density: float32 [8, 256, 1024], P('inst', 'space'), may hold values from 0.8 to 1.25
- velocity: float32 [3, 8, 256, 1024], P(None, 'inst', 'space'), may hold values from -0.6 to 0.6
- pressure: float32 [8, 256, 1024], P('inst', 'space'), may hold values from 0.5 to 1
- obs_pos: float32 [3, 512], P(None, 'space'), may hold values from -16 to 16, as said below
- obs_weight: float32 [2, 512], P(None, 'space'), may hold values from -0.6 to 0.6
- obs_harmonic: int32 [512], P('space'), may hold values from 1 to 3
- panel_pos: float32 [3, 65536], replicated, may hold values from -1 to 1
- panel_normal: float32 [3, 65536], P(None, 'space'), may hold values from -5 to 5
- panel_cell: int32 [65536], P('space'), may hold values from 0 to 8191
- plane_nbr: int32 [4, 1024], replicated, may hold values from 0 to 1023
Outputs:
- adjoint: float32 [5, 8, 256, 1024], P(None, 'inst', 'space')
Inputs may be any that keep to these rules, and one draw needn't show every extreme that they name: `obs_pos`: observers lie between 8 and 16 from the anchor, outside the panels' cube. panel_cell[q] is an index into the 8 x 1024 cells of the slot's owner, layer panel_cell[q] // 1024.
All inputs are finite; a program needn't handle non-finite values.
Results may differ from a plain program's by a relative error of at most 0.0001.
Values sent between devices are 32-bit elements; how exact they have to be, the bound alone decides.
A program may use at most 64 MiB of HBM per device.

v0:
```python
import math
import jax
import jax.numpy as jnp
from jax import lax
from jax.sharding import PartitionSpec as P

ITERS = 3
GAMMA = 1.4
KWAVE = 0.7
RADIUS = 10.0
TAU = 0.05
DISSIP = 0.25
OMEGA = 1.5
VISCO = 0.5


def padded_2(cells, sides, width):
    for axis, dim in sides:
        count = lax.axis_size(axis)
        head = lax.slice_in_dim(cells, 0, width, axis=dim)
        tail = lax.slice_in_dim(cells, cells.shape[dim] - width, cells.shape[dim], axis=dim)
        cells = jnp.concatenate(
            [
                lax.ppermute(tail, axis, [(i, (i + 1) % count) for i in range(count)]),
                cells,
                lax.ppermute(head, axis, [((i + 1) % count, i) for i in range(count)]),
            ],
            axis=dim,
        )
    return cells


def panel_block(observers, panels, time_now):
    delta = panels[:, None, :] - observers[:3, :, None]
    dist2 = jnp.sum(delta * delta, axis=0)
    dist = jnp.sqrt(dist2)
    harm = observers[5][:, None]
    phase = harm * (time_now - KWAVE * dist)
    amp = (
        (observers[3][:, None] * jnp.cos(phase) + observers[4][:, None] * jnp.sin(phase))
        * (RADIUS * RADIUS)
        / (dist2 * dist)
    )
    return jnp.sum(amp[None] * delta, axis=1)


def sensitivity(observers, panels, time_now):
    count = panels.shape[1]
    obs_count = observers.shape[1]
    block = math.gcd(count, max(128, 262144 // obs_count))
    split = panels.reshape(3, count // block, block).transpose(1, 0, 2)
    out = lax.map(lambda piece: panel_block(observers, piece, time_now), split)
    return out.transpose(1, 0, 2).reshape(3, count)


def conserved(density, velocity, pressure):
    moment = density[None] * velocity
    energy = pressure / (GAMMA - 1.0) + 0.5 * density * jnp.sum(velocity * velocity, axis=0)
    return jnp.concatenate([density[None], moment, energy[None]], axis=0)


def fluxes(state):
    dens = state[0]
    moment = state[1:4]
    energy = state[4]
    vel = moment / dens
    press = (GAMMA - 1.0) * (energy - 0.5 * jnp.sum(moment * vel, axis=0))
    result = []
    for axis_d in range(3):
        comps = [moment[axis_d]]
        for axis_e in range(3):
            term = moment[axis_e] * vel[axis_d]
            if axis_e == axis_d:
                term = term + press
            comps.append(term)
        comps.append((energy + press) * vel[axis_d])
        result.append(jnp.stack(comps))
    return tuple(result)


def spectral_coeff(offset, count):
    safe = jnp.where(offset == 0, 1.0, offset)
    angle = math.pi * safe / count
    even_odd_flag = 1.0 - 2.0 * jnp.mod(safe, 2.0)
    other = (
        -(OMEGA / 2.0) * even_odd_flag * jnp.cos(angle) / jnp.sin(angle)
        + VISCO * (OMEGA * OMEGA / 2.0) * even_odd_flag / jnp.sin(angle) ** 2
    )
    return jnp.where(offset == 0, VISCO * OMEGA * OMEGA * (count * count + 2.0) / 12.0, other)


def shards(
    psi_start,
    density,
    velocity,
    pressure,
    obs_pos,
    obs_weight,
    obs_harmonic,
    panel_pos,
    panel_normal,
    panel_cell,
    plane_nbr,
):
    inst_count = lax.axis_size("inst")
    inst_id = lax.axis_index("inst")
    space_id = lax.axis_index("space")
    time_now = 2.0 * math.pi * inst_id.astype(jnp.float32) / inst_count
    observers = jnp.concatenate(
        [obs_pos, obs_weight, obs_harmonic[None].astype(jnp.float32)], axis=0
    )
    owned_count = panel_normal.shape[1]
    whole = sensitivity(observers, panel_pos, time_now)
    total = lax.psum(whole, "space")
    sens = lax.dynamic_slice_in_dim(total, space_id * owned_count, owned_count, 1)
    weight = jnp.sum(sens * panel_normal, axis=0)
    layers = psi_start.shape[2]
    plane = psi_start.shape[3]
    wall = jax.ops.segment_sum(weight, panel_cell, num_segments=layers * plane).reshape(
        layers, plane
    )
    dens = density[0]
    vel = velocity[:, 0]
    state = conserved(dens, vel, pressure[0])
    slope = jnp.concatenate(
        [0.5 * jnp.sum(vel * vel, axis=0)[None], -vel, jnp.ones_like(dens)[None]], axis=0
    ) * (GAMMA - 1.0)
    source = slope * wall[None]
    _, pull = jax.vjp(fluxes, state)
    psi = psi_start[:, 0]
    for step in range(ITERS):
        padded = padded_2(psi, (("space", 1),), 1)
        minus_a = padded[:, :-2]
        plus_a = padded[:, 2:]
        plus_y = jnp.take(psi, plane_nbr[0], axis=2)
        minus_y = jnp.take(psi, plane_nbr[1], axis=2)
        plus_z = jnp.take(psi, plane_nbr[2], axis=2)
        minus_z = jnp.take(psi, plane_nbr[3], axis=2)
        middle_point = pull(
            (0.5 * (minus_a - plus_a), 0.5 * (minus_y - plus_y), 0.5 * (minus_z - plus_z))
        )[0]
        spread = 6.0 * psi - (minus_a + plus_a + plus_y + minus_y + plus_z + minus_z)
        every_instant = lax.all_gather(psi[:, None], "inst", axis=1, tiled=True)
        others = jnp.arange(inst_count, dtype=jnp.int32)
        row_entry = spectral_coeff(
            jnp.mod(inst_id - others, inst_count).astype(jnp.float32), float(inst_count)
        )
        spectral_operator = jnp.einsum(
            "c,kcyo->kyo", row_entry, every_instant, precision=lax.Precision.HIGHEST
        )
        psi = psi - TAU * (middle_point + DISSIP * spread + spectral_operator + source)
    return psi[:, None]


def solution(mesh):
    placed = (
        P(None, "inst", "space", None),
        P("inst", "space", None),
        P(None, "inst", "space", None),
        P("inst", "space", None),
        P(None, "space"),
        P(None, "space"),
        P("space"),
        P(),
        P(None, "space"),
        P("space"),
        P(),
    )
    return jax.shard_map(
        shards,
        mesh=mesh,
        in_specs=placed,
        out_specs=P(None, "inst", "space", None),
        check_vma=False,
    )
```

profile of v0, /device:TPU:2, one launch (start us, length us, event | category | flops | bytes accessed | tf_op | source)
XLA Modules:
  0.0 505.2 jit_solution(14409982304165432410)
XLA Ops:
  8.0 38.1 %while.10 = (s32[]{:T(128)}, f32[4,3,16384]{2,1,0:T(4,128)}, f32[2,16]{1,0:T(2,128)}, f32[1,16]{1,0:T(1,128)S(1)}, f32[]{:T(128)}, /*index=5*/f32[4,3,16384]{2,1,0:T(4,128)}, f32[3,16]{1,0:T(4,128)}, s32[]{:T(128)}) while((s32[]{:T(128)}, f32[4,3,16384]{2,1,0:T(4,128)}, f32[2,16]{1,0:T(2,128)}, f32[1,16]{1,0:T(1,128)S(1)}, f32[]{:T(128)}, ...), condition=%wide.region_6.8_spmd, body=%wide.region_3.7_spmd.sunk | while | flops 6766594 | bytes 5637533 | solution.py:52
  11.1 4.3 fusion.108
  15.4 1.5 fusion.109
  20.6 4.3 fusion.108
  24.9 1.5 fusion.109
  30.1 4.3 fusion.108
  34.4 1.5 fusion.109
  39.6 4.3 fusion.108
  43.9 1.5 fusion.109
  47.3 6.4 %collective-permute-start.1 = (f32[5,1,1024]{2,1,0:T(1,128)S(1)}, f32[5,1,1024]{2,1,0:T(1,128)S(1)}, u32[]{:S(2)}, u32[]{:S(2)}) collective-permute-start(f32[5,1,1024]{2,1,0:T(1,128)S(1)} %get-tuple-element.159), channel_id=1, source_target_pairs={{1,0},{2,1},{3,2},{4,3},{5,4},{6,5},{7,6},{8,7},{9,8},{10,9},{11,1... | collective-permute-start | bytes 61448 | tf_op jit(solution)/shard_map/ppermute | solution.py:26
  53.8 2.6 copy.184
  56.5 10.4 %gather_fusion = f32[1024,5,8]{2,1,0:T(8,128)} fusion(f32[5,8,1024]{1,0,2:T(8,128)} %copy.184, s32[1024]{0:T(1024)S(1)} %fusion.60), kind=kCustom, calls=%fused_computation.clone | custom fusion | bytes 331776 | tf_op jit(solution)/shard_map/jit(_take)/gather | solution.py:138
  66.9 2.7 copy.185
  69.6 10.4 %gather_fusion.1 = f32[1024,5,8]{2,1,0:T(8,128)} fusion(f32[5,8,1024]{1,0,2:T(8,128)} %copy.184, s32[1024]{0:T(1024)S(1)} %fusion.61), kind=kCustom, calls=%fused_computation.1.clone | custom fusion | bytes 331776 | tf_op jit(solution)/shard_map/jit(_take)/gather | solution.py:137
  79.9 2.6 copy.187
  82.5 10.4 %gather_fusion.2 = f32[1024,5,8]{2,1,0:T(8,128)} fusion(f32[5,8,1024]{1,0,2:T(8,128)} %copy.184, s32[1024]{0:T(1024)S(1)} %fusion.62), kind=kCustom, calls=%fused_computation.2.clone | custom fusion | bytes 331776 | tf_op jit(solution)/shard_map/jit(_take)/gather | solution.py:136
  92.9 2.6 copy.189
  95.6 10.4 %gather_fusion.3 = f32[1024,5,8]{2,1,0:T(8,128)} fusion(f32[5,8,1024]{1,0,2:T(8,128)} %copy.184, s32[1024]{0:T(1024)S(1)} %fusion.63), kind=kCustom, calls=%fused_computation.3.clone | custom fusion | bytes 331776 | tf_op jit(solution)/shard_map/jit(_take)/gather | solution.py:135
  106.0 2.6 copy.191
  109.2 169.2 %all-reduce.80.cloned.1.call-done = f32[3,65536]{1,0:T(4,128)} async-done(((f32[3,65536]{1,0:T(4,128)}), f32[3,65536]{1,0:T(4,128)}) %all-reduce.80.cloned.1.call-update) | async-done | bytes 786448 | tf_op jit(solution)/shard_map/psum | solution.py:114
  279.1 11.6 %scatter_custom_fusion = f32[8192]{0:T(1024)S(1)} fusion(s32[2048]{0:T(1024)} %param.24, f32[2048]{0:T(1024)S(1)} %multiply_reduce_fusion.4, f32[]{:T(128)} %constant.59.clone.1), kind=kCustom, calls=%fused_computation.205 | custom fusion | flops 2048 | bytes 33280 | tf_op jit(solution)/shard_map/scatter-add | solution.py:119
  290.8 3.2 fusion.9
  294.2 2.7 copy.192
  296.8 10.4 %gather_fusion.4 = f32[1024,5,8]{2,1,0:T(8,128)} fusion(f32[5,8,1024]{1,0,2:T(8,128)} %copy.192, s32[1024]{0:T(1024)S(1)} %fusion.60), kind=kCustom, calls=%fused_computation.4.clone | custom fusion | bytes 331776 | tf_op jit(solution)/shard_map/jit(_take)/gather | solution.py:138
  307.2 10.3 %gather_fusion.5 = f32[1024,5,8]{2,1,0:T(8,128)} fusion(f32[5,8,1024]{1,0,2:T(8,128)} %copy.192, s32[1024]{0:T(1024)S(1)} %fusion.61), kind=kCustom, calls=%fused_computation.5.clone | custom fusion | bytes 331776 | tf_op jit(solution)/shard_map/jit(_take)/gather | solution.py:137
  317.5 10.4 %gather_fusion.6 = f32[1024,5,8]{2,1,0:T(8,128)} fusion(f32[5,8,1024]{1,0,2:T(8,128)} %copy.192, s32[1024]{0:T(1024)S(1)} %fusion.62), kind=kCustom, calls=%fused_computation.6.clone | custom fusion | bytes 331776 | tf_op jit(solution)/shard_map/jit(_take)/gather | solution.py:136
  327.9 10.4 %gather_fusion.7 = f32[1024,5,8]{2,1,0:T(8,128)} fusion(f32[5,8,1024]{1,0,2:T(8,128)} %copy.192, s32[1024]{0:T(1024)S(1)} %fusion.63), kind=kCustom, calls=%fused_computation.7.clone | custom fusion | bytes 331776 | tf_op jit(solution)/shard_map/jit(_take)/gather | solution.py:135
  338.3 2.6 copy.193
  340.9 2.6 copy.195
  343.5 2.6 copy.197
  346.2 2.6 copy.199
  349.1 4.1 collective-permute-start.3
  353.3 1.4 collective-permute-done.2
  355.0 37.8 %all-gather.8.cloned.1.call-done = f32[5,64,1024]{2,1,0:T(8,128)} async-done(((f32[5,8,1024]{2,1,0:T(8,128)}), f32[5,64,1024]{2,1,0:T(8,128)}) %all-gather.8.cloned.1.call-update) | async-done | bytes 1310736 | tf_op jit(solution)/shard_map/all_gather | solution.py:143
  392.8 3.2 fusion.7
  396.2 2.7 copy.200
  398.8 10.4 %gather_fusion.8 = f32[1024,5,8]{2,1,0:T(8,128)} fusion(f32[5,8,1024]{1,0,2:T(8,128)} %copy.200, s32[1024]{0:T(1024)S(1)} %fusion.60), kind=kCustom, calls=%fused_computation.8.clone | custom fusion | bytes 331776 | tf_op jit(solution)/shard_map/jit(_take)/gather | solution.py:138
  409.2 10.3 %gather_fusion.9 = f32[1024,5,8]{2,1,0:T(8,128)} fusion(f32[5,8,1024]{1,0,2:T(8,128)} %copy.200, s32[1024]{0:T(1024)S(1)} %fusion.61), kind=kCustom, calls=%fused_computation.9.clone | custom fusion | bytes 331776 | tf_op jit(solution)/shard_map/jit(_take)/gather | solution.py:137
  419.5 10.4 %gather_fusion.10 = f32[1024,5,8]{2,1,0:T(8,128)} fusion(f32[5,8,1024]{1,0,2:T(8,128)} %copy.200, s32[1024]{0:T(1024)S(1)} %fusion.62), kind=kCustom, calls=%fused_computation.10.clone | custom fusion | bytes 331776 | tf_op jit(solution)/shard_map/jit(_take)/gather | solution.py:136
  429.9 10.4 %gather_fusion.11 = f32[1024,5,8]{2,1,0:T(8,128)} fusion(f32[5,8,1024]{1,0,2:T(8,128)} %copy.200, s32[1024]{0:T(1024)S(1)} %fusion.63), kind=kCustom, calls=%fused_computation.11.clone | custom fusion | bytes 331776 | tf_op jit(solution)/shard_map/jit(_take)/gather | solution.py:135
  440.3 2.6 copy.201
  442.9 2.6 copy.203
  445.5 2.6 copy.205
  448.1 2.6 copy.207
  451.1 3.8 collective-permute-start.5
  455.0 1.5 collective-permute-done.4
  456.8 36.8 %all-gather.10.cloned.1.call-done = f32[5,64,1024]{2,1,0:T(8,128)} async-done(((f32[5,8,1024]{2,1,0:T(8,128)}), f32[5,64,1024]{2,1,0:T(8,128)}) %all-gather.10.cloned.1.call-update) | async-done | bytes 1310736 | tf_op jit(solution)/shard_map/all_gather | solution.py:143
  493.6 3.2 fusion.5
  (105 shorter events, 20.9 us)
Async XLA Ops:
  7.4 270.9 %all-reduce.80.cloned.1.call-start = ((), (), s32[]{:S(2)}) async-start(), calls=%async_computation.1 | async-start | bytes 2097152 | tf_op jit(solution)/shard_map/psum | solution.py:114
  8.0 45.8 %copy-start.4 = (f32[5,1,8,1024]{3,2,1,0:T(8,128)S(1)}, f32[5,1,8,1024]{3,2,1,0:T(8,128)}, u32[]{:S(2)}) copy-start(f32[5,1,8,1024]{3,2,1,0:T(8,128)} %param.15) | copy-start | bytes 491524
  46.1 10.3 %copy-start.9 = (s32[4,1024]{1,0:T(4,128)S(1)}, s32[4,1024]{1,0:T(4,128)}, u32[]{:S(2)}) copy-start(s32[4,1024]{1,0:T(4,128)} %param.25) | copy-start | bytes 49156
  46.2 244.6 %all-gather.6.cloned.1.call-start = ((), (), s32[]{:S(2)}) async-start(), calls=%async_computation | async-start | bytes 1474560 | tf_op jit(solution)/shard_map/all_gather | solution.py:143
  47.3 61.6 %collective-permute-start = (f32[5,1,1024]{2,1,0:T(1,128)S(1)}, f32[5,1,1024]{2,1,0:T(1,128)S(1)}, u32[]{:S(2)}, u32[]{:S(2)}) collective-permute-start(f32[5,1,1024]{2,1,0:T(1,128)S(1)} %get-tuple-element.160), channel_id=1, source_target_pairs={{0,1},{1,2},{2,3},{3,4},{4,5},{5,6},{6,7},{7,8},{8,9},{9,10},{10,1... | collective-permute-start | bytes 61448 | tf_op jit(solution)/shard_map/ppermute | solution.py:24
  47.3 61.5 %collective-permute-start.1 = (f32[5,1,1024]{2,1,0:T(1,128)S(1)}, f32[5,1,1024]{2,1,0:T(1,128)S(1)}, u32[]{:S(2)}, u32[]{:S(2)}) collective-permute-start(f32[5,1,1024]{2,1,0:T(1,128)S(1)} %get-tuple-element.159), channel_id=1, source_target_pairs={{1,0},{2,1},{3,2},{4,3},{5,4},{6,5},{7,6},{8,7},{9,8},{10,9},{11,1... | collective-permute-start | bytes 61448 | tf_op jit(solution)/shard_map/ppermute | solution.py:26
  53.8 339.0 %all-gather.8.cloned.1.call-start = ((), (), s32[]{:S(2)}) async-start(), calls=%async_computation.2 | async-start | bytes 1474560 | tf_op jit(solution)/shard_map/all_gather | solution.py:143
  92.9 15.7 %copy-start.5 = (f32[1,8,1024]{2,1,0:T(8,128)S(1)}, f32[1,8,1024]{2,1,0:T(8,128)}, u32[]{:S(2)}) copy-start(f32[1,8,1024]{2,1,0:T(8,128)} %param.16) | copy-start | bytes 98308
  92.9 15.7 %copy-start.6 = (f32[3,1,8,1024]{3,2,1,0:T(8,128)S(1)}, f32[3,1,8,1024]{3,2,1,0:T(8,128)}, u32[]{:S(2)}) copy-start(f32[3,1,8,1024]{3,2,1,0:T(8,128)} %param.17) | copy-start | bytes 294916
  92.9 15.8 %copy-start.7 = (f32[1,8,1024]{2,1,0:T(8,128)S(1)}, f32[1,8,1024]{2,1,0:T(8,128)}, u32[]{:S(2)}) copy-start(f32[1,8,1024]{2,1,0:T(8,128)} %param.18) | copy-start | bytes 98308
  106.0 3.0 copy-start.10
  106.0 172.4 %copy-start.8 = (f32[3,2048]{1,0:T(4,128)S(1)}, f32[3,2048]{1,0:T(4,128)}, u32[]{:S(2)}) copy-start(f32[3,2048]{1,0:T(4,128)} %param.23) | copy-start | bytes 73732
  294.1 44.1 %copy-start.2 = (f32[5,8,1024]{2,1,0:T(8,128)}, f32[5,8,1024]{2,1,0:T(8,128)S(1)}, u32[]{:S(2)}) copy-start(f32[5,8,1024]{2,1,0:T(8,128)S(1)} %fusion.36) | copy-start | bytes 491524
  338.3 155.3 %all-gather.10.cloned.1.call-start = ((), (), s32[]{:S(2)}) async-start(), calls=%async_computation.3 | async-start | bytes 1474560 | tf_op jit(solution)/shard_map/all_gather | solution.py:143
  343.5 5.2 %copy-start.3 = (f32[5,8,1024]{2,1,0:T(8,128)S(1)}, f32[5,8,1024]{2,1,0:T(8,128)}, u32[]{:S(2)}) copy-start(f32[5,8,1024]{2,1,0:T(8,128)} %copy-done.2) | copy-start | bytes 491524
  348.8 5.8 %collective-permute-start.2 = (f32[5,1,1024]{2,1,0:T(1,128)S(1)}, f32[5,1,1024]{2,1,0:T(1,128)S(1)}, u32[]{:S(2)}, u32[]{:S(2)}) collective-permute-start(f32[5,1,1024]{2,1,0:T(1,128)S(1)} %get-tuple-element.148), channel_id=1, source_target_pairs={{0,1},{1,2},{2,3},{3,4},{4,5},{5,6},{6,7},{7,8},{8,9},{9,10},{10,1... | collective-permute-start | bytes 61448 | tf_op jit(solution)/shard_map/ppermute | solution.py:24
  349.1 5.6 %collective-permute-start.3 = (f32[5,1,1024]{2,1,0:T(1,128)S(1)}, f32[5,1,1024]{2,1,0:T(1,128)S(1)}, u32[]{:S(2)}, u32[]{:S(2)}) collective-permute-start(f32[5,1,1024]{2,1,0:T(1,128)S(1)} %get-tuple-element.147), channel_id=1, source_target_pairs={{1,0},{2,1},{3,2},{4,3},{5,4},{6,5},{7,6},{8,7},{9,8},{10,9},{11,1... | collective-permute-start | bytes 61448 | tf_op jit(solution)/shard_map/ppermute | solution.py:26
  396.2 44.1 %copy-start = (f32[5,8,1024]{2,1,0:T(8,128)}, f32[5,8,1024]{2,1,0:T(8,128)S(1)}, u32[]{:S(2)}) copy-start(f32[5,8,1024]{2,1,0:T(8,128)S(1)} %fusion.25) | copy-start | bytes 491524
  445.5 5.2 %copy-start.1 = (f32[5,8,1024]{2,1,0:T(8,128)S(1)}, f32[5,8,1024]{2,1,0:T(8,128)}, u32[]{:S(2)}) copy-start(f32[5,8,1024]{2,1,0:T(8,128)} %copy-done) | copy-start | bytes 491524
  450.8 5.7 %collective-permute-start.4 = (f32[5,1,1024]{2,1,0:T(1,128)S(1)}, f32[5,1,1024]{2,1,0:T(1,128)S(1)}, u32[]{:S(2)}, u32[]{:S(2)}) collective-permute-start(f32[5,1,1024]{2,1,0:T(1,128)S(1)} %get-tuple-element.137), channel_id=1, source_target_pairs={{0,1},{1,2},{2,3},{3,4},{4,5},{5,6},{6,7},{7,8},{8,9},{9,10},{10,1... | collective-permute-start | bytes 61448 | tf_op jit(solution)/shard_map/ppermute | solution.py:24
  451.1 5.4 %collective-permute-start.5 = (f32[5,1,1024]{2,1,0:T(1,128)S(1)}, f32[5,1,1024]{2,1,0:T(1,128)S(1)}, u32[]{:S(2)}, u32[]{:S(2)}) collective-permute-start(f32[5,1,1024]{2,1,0:T(1,128)S(1)} %get-tuple-element.136), channel_id=1, source_target_pairs={{1,0},{2,1},{3,2},{4,3},{5,4},{6,5},{7,6},{8,7},{9,8},{10,9},{11,1... | collective-permute-start | bytes 61448 | tf_op jit(solution)/shard_map/ppermute | solution.py:26
Sparse Core Ops, SparseCore 0:
  46.3 231.9 all-reduce.79
Sparse Core Ops, SparseCore 1:
  53.8 54.9 all-gather.5
  338.4 54.4 all-gather.7
  440.4 53.2 all-gather.9
where the time goes:
time: 506 us; the launch traced here: 505 us
  waiting for transfers between devices  247 us (49%)
  local copies, waits for them, and re-layouts  175 us (35%)
  other arithmetic  43.5 us (9%)
  between operations  15.5 us (3%)
  starting transfers between devices  15.1 us (3%)
  matrix products  9.46 us (2%)
    psum x1, waiting for transfers between devices, shards(): total = lax.psum(whole, 'space')  169 us
    all_gather x3, waiting for transfers between devices, shards(): every_instant = lax.all_gather(psi[:, None], 'inst', axis=1, tiled=True)  74.7 us
    gather x6, local copies, waits for them, and re-layouts, shards(): minus_y = jnp.take(psi, plane_nbr[1], axis=2)  39.1 us
    gather x6, local copies, waits for them, and re-layouts, shards(): plus_y = jnp.take(psi, plane_nbr[0], axis=2)  39 us
    gather x6, local copies, waits for them, and re-layouts, shards(): minus_z = jnp.take(psi, plane_nbr[3], axis=2)  38.9 us
    gather x6, local copies, waits for them, and re-layouts, shards(): plus_z = jnp.take(psi, plane_nbr[2], axis=2)  38.8 us
    div x4, other arithmetic, panel_block(): (observers[3][:, None] * jnp.cos(phase) + observers[4][:, None] * jnp.sin...  17.3 us
    ppermute x3, starting transfers between devices, padded_2(): lax.ppermute(head, axis, [((i + 1) % count, i) for i in range(count)])  14.3 us
  transfers between devices with their start and end apart: 10, of which 5 were waited for; matrix products, arithmetic and copies ran while one was open for 18% of the time, Pallas kernels for 0%

commit v1 on v0

--- a/solution.py
+++ b/solution.py
@@ -1,3 +1,4 @@
+import functools
 import math
 import jax
 import jax.numpy as jnp
@@ -12,6 +13,14 @@
 DISSIP = 0.25
 OMEGA = 1.5
 VISCO = 0.5
+
+
+def _map_lots_all(vector, axis_id):
+    v_now = jnp.sum(jax.lax.all_gather(vector, axis_name=axis_id), axis=0)
+    return v_now
+
+
+plan_forms = functools.partial(_map_lots_all, axis_id="space")
 
 
 def padded_2(cells, sides, width):
@@ -111,7 +120,7 @@
     )
     owned_count = panel_normal.shape[1]
     whole = sensitivity(observers, panel_pos, time_now)
-    total = lax.psum(whole, "space")
+    total = plan_forms(whole)
     sens = lax.dynamic_slice_in_dim(total, space_id * owned_count, owned_count, 1)
     weight = jnp.sum(sens * panel_normal, axis=0)
     layers = psi_start.shape[2]

time: 506 us -> 412 us (0.81)
  waiting for transfers between devices: 247 us -> 141 us
  other arithmetic: 43.5 us -> 55.5 us
    psum x1 -> x0, waiting for transfers between devices: 169 us -> none  [shards(): total = lax.psum(whole, 'space')]
    all_gather x0 -> x1, waiting for transfers between devices: none -> 140 us  [_map_lots_all(): v_now = jnp.sum(jax.lax.all_gather(vector, axis_name=axis_id), axis=0)]
    all_gather x3, waiting for transfers between devices: 74.7 us -> 0.06 us  [shards(): every_instant = lax.all_gather(psi[:, None], 'inst', axis=1, tiled=True)]
    reduce_sum x0 -> x1, other arithmetic: none -> 11.5 us  [_map_lots_all(): v_now = jnp.sum(jax.lax.all_gather(vector, axis_name=axis_id), axis=0)]
  transfers between devices with their start and end apart: 10 -> 10, of which waited for: 5 -> 1; matrix products, arithmetic and copies ran while one was open for 18% -> 51% of each run, Pallas kernels for 0% -> 0%
where the time goes in v1:
time: 412 us; the launch traced here: 411 us
  local copies, waits for them, and re-layouts  177 us (43%)
  waiting for transfers between devices  141 us (34%)
  other arithmetic  55.5 us (13%)
  starting transfers between devices  14.4 us (3%)
  between operations  13.6 us (3%)
  matrix products  9.5 us (2%)
    all_gather x1, waiting for transfers between devices, _map_lots_all(): v_now = jnp.sum(jax.lax.all_gather(vector, axis_name=axis_id), axis=0)  140 us
    gather x6, local copies, waits for them, and re-layouts, shards(): minus_y = jnp.take(psi, plane_nbr[1], axis=2)  39.5 us
    gather x6, local copies, waits for them, and re-layouts, shards(): minus_z = jnp.take(psi, plane_nbr[3], axis=2)  39.3 us
    gather x6, local copies, waits for them, and re-layouts, shards(): plus_y = jnp.take(psi, plane_nbr[0], axis=2)  39 us
    gather x6, local copies, waits for them, and re-layouts, shards(): plus_z = jnp.take(psi, plane_nbr[2], axis=2)  39 us
    div x4, other arithmetic, panel_block(): (observers[3][:, None] * jnp.cos(phase) + observers[4][:, None] * jnp.sin...  17.4 us
    ppermute x3, starting transfers between devices, padded_2(): lax.ppermute(head, axis, [((i + 1) % count, i) for i in range(count)])  14.3 us
    reduce_sum x1, other arithmetic, _map_lots_all(): v_now = jnp.sum(jax.lax.all_gather(vector, axis_name=axis_id), axis=0)  11.5 us
  transfers between devices with their start and end apart: 10, of which 1 were waited for; matrix products, arithmetic and copies ran while one was open for 51% of the time, Pallas kernels for 0%

profile of v1, /device:TPU:2, one launch (start us, length us, event | category | flops | bytes accessed | tf_op | source)
XLA Modules:
  0.0 411.0 jit_solution(11977329365380571743)
XLA Ops:
  8.0 38.2 %while.10 = (s32[]{:T(128)}, f32[4,3,16384]{2,1,0:T(4,128)}, f32[2,16]{1,0:T(2,128)}, f32[1,16]{1,0:T(1,128)S(1)}, f32[]{:T(128)}, /*index=5*/f32[4,3,16384]{2,1,0:T(4,128)}, f32[3,16]{1,0:T(4,128)}, s32[]{:T(128)}) while((s32[]{:T(128)}, f32[4,3,16384]{2,1,0:T(4,128)}, f32[2,16]{1,0:T(2,128)}, f32[1,16]{1,0:T(1,128)S(1)}, f32[]{:T(128)}, ...), condition=%wide.region_6.8_spmd, body=%wide.region_3.7_spmd.sunk | while | flops 6766594 | bytes 5637033 | solution.py:61
  9.7 1.2 fusion.107
  11.0 4.3 %fusion.108 = f32[16,16384]{1,0:T(8,128)S(1)} fusion(f32[16,16384]{1,0:T(8,128)S(1)} %fusion.107, f32[16]{0:T(128)S(1)} %get-tuple-element.238, f32[]{:T(128)} %get-tuple-element.260, f32[16]{0:T(128)S(1)} %bitcast.221, f32[16]{0:T(128)S(1)} %get-tuple-element.239), kind=kLoop, calls=%fused_computation.21.clone.1 | loop fusion | flops 2359296 | bytes 2097348 | tf_op jit(solution)/shard_map/while/body/eval_jaxpr/div | solution.py:49
  15.3 1.5 fusion.109
  19.3 1.2 fusion.107
  20.5 4.3 %fusion.108 = f32[16,16384]{1,0:T(8,128)S(1)} fusion(f32[16,16384]{1,0:T(8,128)S(1)} %fusion.107, f32[16]{0:T(128)S(1)} %get-tuple-element.238, f32[]{:T(128)} %get-tuple-element.260, f32[16]{0:T(128)S(1)} %bitcast.221, f32[16]{0:T(128)S(1)} %get-tuple-element.239), kind=kLoop, calls=%fused_computation.21.clone.1 | loop fusion | flops 2359296 | bytes 2097348 | tf_op jit(solution)/shard_map/while/body/eval_jaxpr/div | solution.py:49
  24.8 1.5 fusion.109
  30.0 4.3 %fusion.108 = f32[16,16384]{1,0:T(8,128)S(1)} fusion(f32[16,16384]{1,0:T(8,128)S(1)} %fusion.107, f32[16]{0:T(128)S(1)} %get-tuple-element.238, f32[]{:T(128)} %get-tuple-element.260, f32[16]{0:T(128)S(1)} %bitcast.221, f32[16]{0:T(128)S(1)} %get-tuple-element.239), kind=kLoop, calls=%fused_computation.21.clone.1 | loop fusion | flops 2359296 | bytes 2097348 | tf_op jit(solution)/shard_map/while/body/eval_jaxpr/div | solution.py:49
  34.4 1.5 fusion.109
  38.4 1.2 fusion.107
  39.6 4.3 %fusion.108 = f32[16,16384]{1,0:T(8,128)S(1)} fusion(f32[16,16384]{1,0:T(8,128)S(1)} %fusion.107, f32[16]{0:T(128)S(1)} %get-tuple-element.238, f32[]{:T(128)} %get-tuple-element.260, f32[16]{0:T(128)S(1)} %bitcast.221, f32[16]{0:T(128)S(1)} %get-tuple-element.239), kind=kLoop, calls=%fused_computation.21.clone.1 | loop fusion | flops 2359296 | bytes 2097348 | tf_op jit(solution)/shard_map/while/body/eval_jaxpr/div | solution.py:49
  43.9 1.5 fusion.109
  46.3 6.4 %collective-permute-start.1 = (f32[5,1,1024]{2,1,0:T(1,128)S(1)}, f32[5,1,1024]{2,1,0:T(1,128)S(1)}, u32[]{:S(2)}, u32[]{:S(2)}) collective-permute-start(f32[5,1,1024]{2,1,0:T(1,128)S(1)} %get-tuple-element.159), channel_id=1, source_target_pairs={{1,0},{2,1},{3,2},{4,3},{5,4},{6,5},{7,6},{8,7},{9,8},{10,9},{11,1... | collective-permute-start | bytes 61448 | tf_op jit(solution)/shard_map/ppermute | solution.py:35
  52.7 2.7 copy.184
  55.4 10.4 %gather_fusion.3 = f32[1024,5,8]{2,1,0:T(8,128)} fusion(f32[5,8,1024]{1,0,2:T(8,128)} %copy.184, s32[1024]{0:T(1024)S(1)} %fusion.63), kind=kCustom, calls=%fused_computation.3.clone | custom fusion | bytes 331776 | tf_op jit(solution)/shard_map/jit(_take)/gather | solution.py:144
  65.8 2.6 copy.191
  68.4 10.4 %gather_fusion.2 = f32[1024,5,8]{2,1,0:T(8,128)} fusion(f32[5,8,1024]{1,0,2:T(8,128)} %copy.184, s32[1024]{0:T(1024)S(1)} %fusion.62), kind=kCustom, calls=%fused_computation.2.clone | custom fusion | bytes 331776 | tf_op jit(solution)/shard_map/jit(_take)/gather | solution.py:145
  78.8 3.3 copy.189
  82.0 10.4 %gather_fusion.1 = f32[1024,5,8]{2,1,0:T(8,128)} fusion(f32[5,8,1024]{1,0,2:T(8,128)} %copy.184, s32[1024]{0:T(1024)S(1)} %fusion.61), kind=kCustom, calls=%fused_computation.1.clone | custom fusion | bytes 331776 | tf_op jit(solution)/shard_map/jit(_take)/gather | solution.py:146
  92.4 2.6 copy.187
  95.1 10.4 %gather_fusion = f32[1024,5,8]{2,1,0:T(8,128)} fusion(f32[5,8,1024]{1,0,2:T(8,128)} %copy.184, s32[1024]{0:T(1024)S(1)} %fusion.60), kind=kCustom, calls=%fused_computation.clone | custom fusion | bytes 331776 | tf_op jit(solution)/shard_map/jit(_take)/gather | solution.py:147
  105.4 2.7 copy.185
  108.7 3.2 fusion.9
  111.9 140.4 %all-gather.9.cloned.1.call-done = f32[32,3,65536]{2,1,0:T(4,128)} async-done(((f32[1,3,65536]{2,1,0:T(4,128)}), f32[32,3,65536]{2,1,0:T(4,128)}) %all-gather.9.cloned.1.call-update) | async-done | bytes 25165840 | tf_op jit(solution)/shard_map/all_gather | solution.py:19
  252.3 11.5 %reduce_sum.92 = f32[3,65536]{1,0:T(4,128)S(1)} reduce(f32[32,3,65536]{2,1,0:T(4,128)} %all-gather.9.cloned.1.call-done, f32[]{:T(128)} %constant.59.clone.1), dimensions={0}, to_apply=%region_7.9 | reduce | flops 6094848 | bytes 25952260 | tf_op jit(solution)/shard_map/reduce_sum | solution.py:19
  263.8 11.4 %scatter_custom_fusion = f32[8192]{0:T(1024)S(1)} fusion(s32[2048]{0:T(1024)} %param.24, f32[2048]{0:T(1024)S(1)} %multiply_reduce_fusion.4, f32[]{:T(128)} %constant.59.clone.1), kind=kCustom, calls=%fused_computation.205 | custom fusion | flops 2048 | bytes 33280 | tf_op jit(solution)/shard_map/scatter-add | solution.py:128
  276.2 3.5 copy.192
  279.7 10.4 %gather_fusion.7 = f32[1024,5,8]{2,1,0:T(8,128)} fusion(f32[5,8,1024]{1,0,2:T(8,128)} %copy.192, s32[1024]{0:T(1024)S(1)} %fusion.63), kind=kCustom, calls=%fused_computation.7.clone | custom fusion | bytes 331776 | tf_op jit(solution)/shard_map/jit(_take)/gather | solution.py:144
  290.1 10.3 %gather_fusion.6 = f32[1024,5,8]{2,1,0:T(8,128)} fusion(f32[5,8,1024]{1,0,2:T(8,128)} %copy.192, s32[1024]{0:T(1024)S(1)} %fusion.62), kind=kCustom, calls=%fused_computation.6.clone | custom fusion | bytes 331776 | tf_op jit(solution)/shard_map/jit(_take)/gather | solution.py:145
  300.5 10.4 %gather_fusion.5 = f32[1024,5,8]{2,1,0:T(8,128)} fusion(f32[5,8,1024]{1,0,2:T(8,128)} %copy.192, s32[1024]{0:T(1024)S(1)} %fusion.61), kind=kCustom, calls=%fused_computation.5.clone | custom fusion | bytes 331776 | tf_op jit(solution)/shard_map/jit(_take)/gather | solution.py:146
  310.9 10.5 %gather_fusion.4 = f32[1024,5,8]{2,1,0:T(8,128)} fusion(f32[5,8,1024]{1,0,2:T(8,128)} %copy.192, s32[1024]{0:T(1024)S(1)} %fusion.60), kind=kCustom, calls=%fused_computation.4.clone | custom fusion | bytes 331776 | tf_op jit(solution)/shard_map/jit(_take)/gather | solution.py:147
  321.4 4.0 collective-permute-start.3
  325.4 2.6 copy.199
  328.0 2.6 copy.197
  330.6 2.6 copy.195
  333.2 2.6 copy.193
  336.3 3.2 fusion.7
  340.3 3.5 copy.200
  343.9 10.4 %gather_fusion.11 = f32[1024,5,8]{2,1,0:T(8,128)} fusion(f32[5,8,1024]{1,0,2:T(8,128)} %copy.200, s32[1024]{0:T(1024)S(1)} %fusion.63), kind=kCustom, calls=%fused_computation.11.clone | custom fusion | bytes 331776 | tf_op jit(solution)/shard_map/jit(_take)/gather | solution.py:144
  354.3 10.3 %gather_fusion.10 = f32[1024,5,8]{2,1,0:T(8,128)} fusion(f32[5,8,1024]{1,0,2:T(8,128)} %copy.200, s32[1024]{0:T(1024)S(1)} %fusion.62), kind=kCustom, calls=%fused_computation.10.clone | custom fusion | bytes 331776 | tf_op jit(solution)/shard_map/jit(_take)/gather | solution.py:145
  364.6 10.4 %gather_fusion.9 = f32[1024,5,8]{2,1,0:T(8,128)} fusion(f32[5,8,1024]{1,0,2:T(8,128)} %copy.200, s32[1024]{0:T(1024)S(1)} %fusion.61), kind=kCustom, calls=%fused_computation.9.clone | custom fusion | bytes 331776 | tf_op jit(solution)/shard_map/jit(_take)/gather | solution.py:146
  375.0 10.5 %gather_fusion.8 = f32[1024,5,8]{2,1,0:T(8,128)} fusion(f32[5,8,1024]{1,0,2:T(8,128)} %copy.200, s32[1024]{0:T(1024)S(1)} %fusion.60), kind=kCustom, calls=%fused_computation.8.clone | custom fusion | bytes 331776 | tf_op jit(solution)/shard_map/jit(_take)/gather | solution.py:147
  385.6 3.9 collective-permute-start.5
  389.5 2.6 copy.207
  392.1 2.6 copy.205
  394.7 2.6 copy.203
  397.3 2.6 copy.201
  400.4 3.2 fusion.5
  (102 shorter events, 16.9 us)
Async XLA Ops:
  6.5 102.2 %all-gather.7.cloned.1.call-start = ((), (), s32[]{:S(2)}) async-start(), calls=%async_computation | async-start | bytes 1474560 | tf_op jit(solution)/shard_map/all_gather | solution.py:152
  7.3 245.0 %all-gather.9.cloned.1.call-start = ((), (), s32[]{:S(2)}) async-start(), calls=%async_computation.1 | async-start | bytes 34603008 | tf_op jit(solution)/shard_map/all_gather | solution.py:19
  8.0 38.2 %copy-start.2 = (f32[5,1,8,1024]{3,2,1,0:T(8,128)S(1)}, f32[5,1,8,1024]{3,2,1,0:T(8,128)}, u32[]{:S(2)}) copy-start(f32[5,1,8,1024]{3,2,1,0:T(8,128)} %param.15) | copy-start | bytes 491524
  46.1 9.2 %copy-start.7 = (s32[4,1024]{1,0:T(4,128)S(1)}, s32[4,1024]{1,0:T(4,128)}, u32[]{:S(2)}) copy-start(s32[4,1024]{1,0:T(4,128)} %param.25) | copy-start | bytes 49156
  46.2 290.1 %all-gather.11.cloned.1.call-start = ((), (), s32[]{:S(2)}) async-start(), calls=%async_computation.2 | async-start | bytes 1474560 | tf_op jit(solution)/shard_map/all_gather | solution.py:152
  46.3 62.1 %collective-permute-start.1 = (f32[5,1,1024]{2,1,0:T(1,128)S(1)}, f32[5,1,1024]{2,1,0:T(1,128)S(1)}, u32[]{:S(2)}, u32[]{:S(2)}) collective-permute-start(f32[5,1,1024]{2,1,0:T(1,128)S(1)} %get-tuple-element.159), channel_id=1, source_target_pairs={{1,0},{2,1},{3,2},{4,3},{5,4},{6,5},{7,6},{8,7},{9,8},{10,9},{11,1... | collective-permute-start | bytes 61448 | tf_op jit(solution)/shard_map/ppermute | solution.py:35
  52.7 55.7 %collective-permute-start = (f32[5,1,1024]{2,1,0:T(1,128)S(1)}, f32[5,1,1024]{2,1,0:T(1,128)S(1)}, u32[]{:S(2)}, u32[]{:S(2)}) collective-permute-start(f32[5,1,1024]{2,1,0:T(1,128)S(1)} %get-tuple-element.160), channel_id=1, source_target_pairs={{0,1},{1,2},{2,3},{3,4},{4,5},{5,6},{6,7},{7,8},{8,9},{9,10},{10,1... | collective-permute-start | bytes 61448 | tf_op jit(solution)/shard_map/ppermute | solution.py:33
  92.4 15.7 %copy-start.3 = (f32[1,8,1024]{2,1,0:T(8,128)S(1)}, f32[1,8,1024]{2,1,0:T(8,128)}, u32[]{:S(2)}) copy-start(f32[1,8,1024]{2,1,0:T(8,128)} %param.16) | copy-start | bytes 98308
  92.4 15.7 %copy-start.4 = (f32[3,1,8,1024]{3,2,1,0:T(8,128)S(1)}, f32[3,1,8,1024]{3,2,1,0:T(8,128)}, u32[]{:S(2)}) copy-start(f32[3,1,8,1024]{3,2,1,0:T(8,128)} %param.17) | copy-start | bytes 294916
  92.4 15.8 %copy-start.5 = (f32[1,8,1024]{2,1,0:T(8,128)S(1)}, f32[1,8,1024]{2,1,0:T(8,128)}, u32[]{:S(2)}) copy-start(f32[1,8,1024]{2,1,0:T(8,128)} %param.18) | copy-start | bytes 98308
  105.4 3.1 copy-start.8
  111.9 151.8 %copy-start.6 = (f32[3,2048]{1,0:T(4,128)S(1)}, f32[3,2048]{1,0:T(4,128)}, u32[]{:S(2)}) copy-start(f32[3,2048]{1,0:T(4,128)} %param.23) | copy-start | bytes 73732
  276.1 45.2 %copy-start.1 = (f32[5,8,1024]{2,1,0:T(8,128)S(1)}, f32[5,8,1024]{2,1,0:T(8,128)}, u32[]{:S(2)}) copy-start(f32[5,8,1024]{2,1,0:T(8,128)} %fusion.36) | copy-start | bytes 491524
  276.2 124.2 %all-gather.13.cloned.1.call-start = ((), (), s32[]{:S(2)}) async-start(), calls=%async_computation.3 | async-start | bytes 1474560 | tf_op jit(solution)/shard_map/all_gather | solution.py:152
  321.4 14.5 %collective-permute-start.3 = (f32[5,1,1024]{2,1,0:T(1,128)S(1)}, f32[5,1,1024]{2,1,0:T(1,128)S(1)}, u32[]{:S(2)}, u32[]{:S(2)}) collective-permute-start(f32[5,1,1024]{2,1,0:T(1,128)S(1)} %get-tuple-element.147), channel_id=1, source_target_pairs={{1,0},{2,1},{3,2},{4,3},{5,4},{6,5},{7,6},{8,7},{9,8},{10,9},{11,1... | collective-permute-start | bytes 61448 | tf_op jit(solution)/shard_map/ppermute | solution.py:35
  325.4 10.5 %collective-permute-start.2 = (f32[5,1,1024]{2,1,0:T(1,128)S(1)}, f32[5,1,1024]{2,1,0:T(1,128)S(1)}, u32[]{:S(2)}, u32[]{:S(2)}) collective-permute-start(f32[5,1,1024]{2,1,0:T(1,128)S(1)} %get-tuple-element.148), channel_id=1, source_target_pairs={{0,1},{1,2},{2,3},{3,4},{4,5},{5,6},{6,7},{7,8},{8,9},{9,10},{10,1... | collective-permute-start | bytes 61448 | tf_op jit(solution)/shard_map/ppermute | solution.py:33
  340.3 45.2 %copy-start = (f32[5,8,1024]{2,1,0:T(8,128)S(1)}, f32[5,8,1024]{2,1,0:T(8,128)}, u32[]{:S(2)}) copy-start(f32[5,8,1024]{2,1,0:T(8,128)} %fusion.25) | copy-start | bytes 491524
  385.6 14.4 %collective-permute-start.5 = (f32[5,1,1024]{2,1,0:T(1,128)S(1)}, f32[5,1,1024]{2,1,0:T(1,128)S(1)}, u32[]{:S(2)}, u32[]{:S(2)}) collective-permute-start(f32[5,1,1024]{2,1,0:T(1,128)S(1)} %get-tuple-element.136), channel_id=1, source_target_pairs={{1,0},{2,1},{3,2},{4,3},{5,4},{6,5},{7,6},{8,7},{9,8},{10,9},{11,1... | collective-permute-start | bytes 61448 | tf_op jit(solution)/shard_map/ppermute | solution.py:35
  389.5 10.5 %collective-permute-start.4 = (f32[5,1,1024]{2,1,0:T(1,128)S(1)}, f32[5,1,1024]{2,1,0:T(1,128)S(1)}, u32[]{:S(2)}, u32[]{:S(2)}) collective-permute-start(f32[5,1,1024]{2,1,0:T(1,128)S(1)} %get-tuple-element.137), channel_id=1, source_target_pairs={{0,1},{1,2},{2,3},{3,4},{4,5},{5,6},{6,7},{7,8},{8,9},{9,10},{10,1... | collective-permute-start | bytes 61448 | tf_op jit(solution)/shard_map/ppermute | solution.py:33
Sparse Core Ops, SparseCore 0:
  10.0 57.2 all-gather.6
  69.1 183.1 all-gather.8
  276.3 54.1 all-gather.10
  340.5 53.2 all-gather.12
